TPU v7x, 32 devices: a whole 2x2x4 slice. The times are simulated.
32 devices in a mesh: ab: 4 (over y, x), cd: 4 (over z), ij: 2 (over core).
Axes of the slice: x: 2, y: 2, z: 4, core: 2. Of those that a mesh axis runs over, the one named last changes fastest.
Arguments:
- amplitudes: float32 [512, 4096], P('ij', ('cd', 'ab')), may hold values from -6 to 6
- integrals: float32 [256, 256, 256], P(('ab', 'cd')), may hold values from -0.375 to 0.375
- tile_row: int32 [256], P(('ab', 'cd')), may hold values from 0 to 3, as said below
- tile_col: int32 [256], P(('ab', 'cd')), may hold values from 0 to 3
- tile_count: int32 [16], P(('ab', 'cd')), may hold values from 1 to 16, as said below
Outputs:
- residual: float32 [512, 4, 16, 64], P('ij', 'ab', 'cd')
Inputs may be any that keep to these rules, and one draw needn't show every extreme that they name: Within one slab the 16 slots name distinct (tile_row, tile_col) pairs. `tile_count`: in every draw some slab has all 16 slots live.
All inputs are finite; a program needn't handle non-finite values.
Results may differ from a plain program's by a relative error of at most 0.0003.
Values sent between devices are 32-bit elements; how exact they have to be, the bound alone decides.
A program may use at most 128 MiB of HBM per device.

v0:
```python
import math
import jax
import jax.numpy as jnp
from jax import lax
from jax.sharding import PartitionSpec as P


def from_partner(block, axis, bit):
    count = lax.axis_size(axis)
    route = []
    for low in range(count):
        high = low | 1 << bit
        if high != low and high < count:
            route += [(low, high), (high, low)]
    return lax.ppermute(block, axis, route)


def place_rows(chosen, tile_rows, row_picks, block_size):
    terms = jnp.einsum("okf,kef->oke", chosen, tile_rows, precision=lax.Precision.HIGHEST)
    occ_dev, slots, width = terms.shape
    terms = terms.reshape(occ_dev, slots, width // block_size, block_size)
    placed = jnp.einsum("rk,okab->aorb", row_picks, terms, precision=lax.Precision.HIGHEST)
    return placed.reshape(width // block_size, occ_dev, row_picks.shape[0] * block_size)


def per_device(amplitudes, integrals, tile_row, tile_col, tile_count):
    occ_dev = amplitudes.shape[0]
    slots = integrals.shape[0]
    tile_size = integrals.shape[1]
    block_size = math.isqrt(tile_size)
    blocks = lax.axis_size("ab")
    cd_size = lax.axis_size("cd")
    group_size = block_size // cd_size
    live_count = tile_count[0]
    live = jnp.arange(slots, dtype=jnp.int32) < live_count
    row_picks = (
        (tile_row[None, :] == jnp.arange(blocks, dtype=jnp.int32)[:, None]) & live[None, :]
    ).astype(jnp.float32)
    gathered = lax.all_gather(amplitudes, "ab", axis=1, tiled=True)
    columns = gathered.reshape(occ_dev, -1, tile_size)
    chosen = jnp.take(columns, tile_col, axis=1)
    partial_value = place_rows(chosen, integrals, row_picks, block_size)
    summed = lax.psum_scatter(partial_value, "cd", scatter_dimension=0, tiled=True)
    direct = jnp.transpose(summed, (1, 0, 2))
    outgoing = summed.reshape(group_size, occ_dev, blocks, cd_size, group_size)
    outgoing = jnp.transpose(outgoing, (2, 3, 1, 0, 4))
    arrived = lax.all_to_all(
        outgoing.reshape(blocks * cd_size, occ_dev * group_size * group_size),
        ("ab", "cd"),
        split_axis=0,
        concat_axis=0,
        tiled=True,
    )
    arrived = arrived.reshape(blocks, cd_size, occ_dev, group_size, group_size)
    mirrored = jnp.transpose(arrived, (2, 4, 0, 1, 3)).reshape(
        occ_dev, group_size, blocks * block_size
    )
    partner = from_partner(mirrored, "ij", 0)
    return (direct + partner).reshape(occ_dev, 1, group_size, blocks * block_size)


def solution(mesh):
    in_specs = (
        P("ij", ("cd", "ab")),
        P(("ab", "cd"), None, None),
        P(("ab", "cd")),
        P(("ab", "cd")),
        P(("ab", "cd")),
    )
    out_specs = P("ij", "ab", "cd", None)
    return jax.shard_map(
        per_device, mesh=mesh, in_specs=in_specs, out_specs=out_specs, check_vma=False
    )
```

profile of v0, /device:TPU:0, one launch (start us, length us, event | category | flops | bytes accessed | tf_op | source)
XLA Modules:
  0.0 149.9 jit_solution(6584111835509438171)
XLA Ops:
  6.5 0.0 all-gather.2.cloned.1.call-start
  6.5 1.8 %copy.17 = f32[256,256]{0,1:T(8,128)} copy(f32[256,256]{1,0:T(8,128)} %param.5) | data formatting | bytes 524288 | tf_op args[0]
  8.3 0.0 all-gather.2.cloned.1.call-update
  8.3 0.0 reduce-scatter.2.cloned.1.call-start
  9.1 0.7 compare_select_fusion
  9.7 0.7 compare_and_fusion
  10.4 28.0 %all-gather.2.cloned.1.call-done = f32[256,1024]{0,1:T(8,128)} async-done(((f32[256,256]{0,1:T(8,128)}), f32[256,1024]{0,1:T(8,128)}) %all-gather.2.cloned.1.call-update) | async-done | bytes 1048592 | tf_op jit(solution)/shard_map/all_gather | solution.py:39
  38.4 1.6 %copy.18 = f32[256,4,256]{2,0,1:T(8,128)S(1)} copy(f32[256,4,256]{0,2,1:T(8,128)} %bitcast.34) | data formatting | bytes 2097152 | tf_op jit(solution)/shard_map/reshape | solution.py:40
  40.0 2.8 %gather_fusion = f32[16,256,256]{2,1,0:T(8,128)} fusion(f32[256,4,256]{2,0,1:T(8,128)S(1)} %copy.18, s32[1024]{0:T(1024)S(1)} %pad_clamp_fusion), kind=kCustom, calls=%fused_computation | custom fusion | bytes 8388672 | tf_op jit(solution)/shard_map/jit(_take)/gather | solution.py:41
  42.8 0.0 copy-start.1
  42.8 12.3 %fusion = f32[16,256,256]{1,2,0:T(8,128)S(1)} fusion(f32[16,256,256]{2,1,0:T(8,128)} %param.6, f32[16,256,256]{2,1,0:T(8,128)} %gather_fusion, pred[16]{0:T(512)(128)(4,1)S(1)} %compare_and_fusion), kind=kOutput, calls=%fused_computation.1 | convolution fusion | flops 3222274048 | bytes 12582928 | tf_op jit(solution)/shard_map/okf,kef->oke/dot_general | solution.py:19
  55.1 0.0 copy-done.1
  55.1 3.9 %fusion.7 = f32[16,256,4,16]{1,2,3,0:T(4,128)S(1)} fusion(f32[256,16,16,16]{0,3,2,1:T(8,128)S(1)} %bitcast.32, s32[16]{0:T(128)S(1)} %copy-done.1, pred[16]{0:T(512)(128)(4,1)S(1)} %iota_compare_fusion.1), kind=kOutput, calls=%fused_computation.8 | convolution fusion | flops 50331776 | bytes 5242960 | tf_op jit(solution)/shard_map/rk,okab->aorb/dot_general | solution.py:22
  58.9 1.2 copy.20
  60.1 0.0 reduce-scatter.2.cloned.1.call-update
  60.1 27.4 %reduce-scatter.2.cloned.1.call-done = f32[4,256,64]{1,2,0:T(8,128)} async-done(((f32[16,256,64]{1,2,0:T(8,128)}), f32[4,256,64]{1,2,0:T(8,128)}) %reduce-scatter.2.cloned.1.call-update) | async-done | bytes 262160 | tf_op jit(solution)/shard_map/reduce_scatter | solution.py:43
  87.6 1.0 reshape.39
  88.6 5.9 %copy.21 = f32[4,256,4,4,4]{4,0,1,3,2:T(4,128)} copy(f32[4,256,4,4,4]{1,4,3,2,0:T(4,128)S(1)} %reshape.39) | data formatting | bytes 524288 | tf_op jit(solution)/shard_map/reshape | solution.py:45
  94.5 11.3 %all_to_all.8 = f32[16,1,4096]{2,1,0:T(1,128)S(1)} reshape(f32[4,4,256,4,4]{4,3,2,1,0:T(4,128)} %bitcast.30) | data formatting | bytes 524288 | tf_op jit(solution)/shard_map/all_to_all | solution.py:47
  105.8 14.4 %all_to_all.10 = f32[16,1,4096]{2,1,0:T(1,128)S(1)} all-to-all(f32[16,1,4096]{2,1,0:T(1,128)S(1)} %all_to_all.8), channel_id=1, replica_groups=mesh['ab'=4,'cd'=4,'ij'=2] {'ab','cd'}, dimensions={0} | all-to-all | bytes 524288 | tf_op jit(solution)/shard_map/all_to_all | solution.py:47
  120.2 0.6 reduce
  120.8 12.9 %reshape.40 = f32[4,4,256,4,4]{4,3,2,1,0:T(4,128)} reshape(f32[16,4096]{1,0:T(8,128)S(1)} %reduce) | data formatting | bytes 524288 | tf_op jit(solution)/shard_map/reshape | solution.py:54
  133.7 0.0 copy-start
  133.7 6.9 %copy.23 = f32[256,4,4,4,4]{0,4,3,2,1:T(4,128)S(1)} copy(f32[256,4,4,4,4]{1,4,0,3,2:T(4,128)} %bitcast.31) | data formatting | bytes 524288 | tf_op jit(solution)/shard_map/transpose | solution.py:55
  140.6 0.1 reshape.41
  140.7 0.1 collective-permute-start
  140.8 1.5 %collective-permute-done = f32[256,4,64]{0,2,1:T(8,128)S(1)} collective-permute-done((f32[256,4,64]{0,2,1:T(8,128)S(1)}, f32[256,4,64]{0,2,1:T(8,128)S(1)}, u32[]{:S(2)}, u32[]{:S(2)}) %collective-permute-start) | collective-permute-done | bytes 262176 | tf_op jit(solution)/shard_map/ppermute | solution.py:15
  142.3 0.0 copy-done
  142.3 0.7 fusion.10
  (2 shorter events, 0.0 us)
Async XLA Ops:
  6.5 31.9 %all-gather.2.cloned.1.call-start = ((), (), s32[]{:S(2)}) async-start(), calls=%async_computation.2 | async-start | bytes 1310720 | tf_op jit(solution)/shard_map/all_gather | solution.py:39
  8.3 79.2 %reduce-scatter.2.cloned.1.call-start = ((), (), s32[]{:S(2)}) async-start(), calls=%async_computation.3 | async-start | bytes 1310720 | tf_op jit(solution)/shard_map/reduce_scatter | solution.py:43
  42.8 12.3 %copy-start.1 = (s32[16]{0:T(128)S(1)}, s32[16]{0:T(128)}, u32[]{:S(2)}) copy-start(s32[16]{0:T(128)} %param.7) | copy-start | bytes 196
  133.7 8.6 %copy-start = (f32[4,256,64]{1,2,0:T(8,128)S(1)}, f32[4,256,64]{1,2,0:T(8,128)}, u32[]{:S(2)}) copy-start(f32[4,256,64]{1,2,0:T(8,128)} %reduce-scatter.2.cloned.1.call-done) | copy-start | bytes 786436
  140.7 1.6 %collective-permute-start = (f32[256,4,64]{0,2,1:T(8,128)S(1)}, f32[256,4,64]{0,2,1:T(8,128)S(1)}, u32[]{:S(2)}, u32[]{:S(2)}) collective-permute-start(f32[256,4,64]{0,2,1:T(8,128)S(1)} %reshape.41), channel_id=1, source_target_pairs={{0,1},{1,0},{2,3},{3,2},{4,5},{5,4},{6,7},{7,6},{8,9},{9,8},{10,11... | collective-permute-start | bytes 786440 | tf_op jit(solution)/shard_map/ppermute | solution.py:15
Sparse Core Ops, SparseCore 0:
  9.2 29.2 all-gather.1
  60.2 27.2 reduce-scatter.1
where the time goes:
time: 150 us
  waiting for transfers between devices  57 us (38%)
  local copies, waits for them, and re-layouts  45.3 us (30%)
  matrix products  16.2 us (11%)
  blocking collectives  14.4 us (10%)
  between operations  14.1 us (9%)
  other arithmetic  2.69 us (2%)
    all_gather x1, waiting for transfers between devices, per_device(): gathered = lax.all_gather(amplitudes, 'ab', axis=1, tiled=True)  28 us
    reduce_scatter x1, waiting for transfers between devices, per_device(): lax.psum_scatter(partial_value, 'cd', scatter_dimension=0, tiled=True)  27.4 us
    all_to_all x1, blocking collectives, per_device(): lax.all_to_all(outgoing.reshape(blocks * cd_size, occ_dev * group_size *...  14.4 us
    reshape x1, local copies, waits for them, and re-layouts, per_device(): arrived = arrived.reshape(blocks, cd_size, occ_dev, group_size, group_size)  12.9 us
    dot_general x1, matrix products, place_rows(): jnp.einsum('okf,kef->oke', chosen, tile_rows, precision=lax.Precision.HIG...  12.3 us
    all_to_all x1, local copies, waits for them, and re-layouts, per_device(): lax.all_to_all(outgoing.reshape(blocks * cd_size, occ_dev * group_size *...  11.3 us
    reshape x2, local copies, waits for them, and re-layouts, per_device(): outgoing = summed.reshape(group_size, occ_dev, blocks, cd_size, group_size)  6.91 us
    transpose x1, local copies, waits for them, and re-layouts, per_device(): jnp.transpose(arrived, (2, 4, 0, 1, 3))  6.88 us
  transfers between devices with their start and end apart: 3, of which 3 were waited for; matrix products, arithmetic and copies ran while one was open for 1% of the time, Pallas kernels for 0%

commit v1 on v0

--- a/solution.py
+++ b/solution.py
@@ -3,6 +3,18 @@
 import jax.numpy as jnp
 from jax import lax
 from jax.sharding import PartitionSpec as P
+
+
+def cut_along(shard, dim, devices):
+    dims = shard.shape
+    blocks = shard.reshape(*dims[:dim], devices, dims[dim] // devices, *dims[dim + 1 :])
+    return jnp.moveaxis(blocks, dim, 0)
+
+
+def laid_out(blocks, dim):
+    dims = list(blocks.shape[1:])
+    dims[dim] *= blocks.shape[0]
+    return jnp.moveaxis(blocks, 0, dim).reshape(dims)
 
 
 def from_partner(block, axis, bit):
@@ -44,13 +56,15 @@
     direct = jnp.transpose(summed, (1, 0, 2))
     outgoing = summed.reshape(group_size, occ_dev, blocks, cd_size, group_size)
     outgoing = jnp.transpose(outgoing, (2, 3, 1, 0, 4))
-    arrived = lax.all_to_all(
-        outgoing.reshape(blocks * cd_size, occ_dev * group_size * group_size),
-        ("ab", "cd"),
-        split_axis=0,
-        concat_axis=0,
-        tiled=True,
-    )
+    shard = outgoing.reshape(blocks * cd_size, occ_dev * group_size * group_size)
+    devices, here = (lax.axis_size(("ab", "cd")), lax.axis_index(("ab", "cd")))
+    parts = cut_along(shard, 0, devices)
+    outs = [parts[here]]
+    for step in range(1, devices):
+        sent = parts[here ^ step]
+        outs.append(lax.ppermute(sent, ("ab", "cd"), [(i, i ^ step) for i in range(devices)]))
+    parts = jnp.stack(outs)[here ^ jnp.arange(devices)]
+    arrived = laid_out(parts, 0)
     arrived = arrived.reshape(blocks, cd_size, occ_dev, group_size, group_size)
     mirrored = jnp.transpose(arrived, (2, 4, 0, 1, 3)).reshape(
         occ_dev, group_size, blocks * block_size

time: 150 us -> 169 us (1.13)
  starting transfers between devices: 0.11 us -> 26.7 us
  blocking collectives: 14.4 us -> 0 us
  waiting for transfers between devices: 57 us -> 61.4 us
  local copies, waits for them, and re-layouts: 45.3 us -> 47.8 us
    ppermute x0 -> x15, starting transfers between devices: none -> 26.5 us  [per_device(): lax.ppermute(sent, ('ab', 'cd'), [(i, i ^ step) for i in range(devices)])]
    another operation x0 -> x3, local copies, waits for them, and re-layouts: none -> 25.6 us  [the longest x1 12.9 us: per_device(): arrived = arrived.reshape(blocks, cd_size, occ_dev, group_size, group_size)]
    all_to_all x1 -> x0, blocking collectives: 14.4 us -> none  [per_device(): lax.all_to_all(outgoing.reshape(blocks * cd_size, occ_dev * group_size *...]
    reshape x1 -> x0, local copies, waits for them, and re-layouts: 12.9 us -> none  [per_device(): arrived = arrived.reshape(blocks, cd_size, occ_dev, group_size, group_size)]
    all_to_all x1 -> x0, local copies, waits for them, and re-layouts: 11.3 us -> none  [per_device(): lax.all_to_all(outgoing.reshape(blocks * cd_size, occ_dev * group_size *...]
    ppermute x0 -> x15, waiting for transfers between devices: none -> 4.43 us  [per_device(): lax.ppermute(sent, ('ab', 'cd'), [(i, i ^ step) for i in range(devices)])]
  transfers between devices with their start and end apart: 3 -> 18, of which waited for: 3 -> 5; matrix products, arithmetic and copies ran while one was open for 1% -> 1% of each run, Pallas kernels for 0% -> 0%
where the time goes in v1:
time: 169 us; the launch traced here: 168 us
  waiting for transfers between devices  61.4 us (36%)
  local copies, waits for them, and re-layouts  47.8 us (28%)
  starting transfers between devices  26.7 us (16%)
  matrix products  16.1 us (10%)
  between operations  14.3 us (8%)
  other arithmetic  2.09 us (1%)
    all_gather x1, waiting for transfers between devices, per_device(): gathered = lax.all_gather(amplitudes, 'ab', axis=1, tiled=True)  28 us
    reduce_scatter x1, waiting for transfers between devices, per_device(): lax.psum_scatter(partial_value, 'cd', scatter_dimension=0, tiled=True)  27.4 us
    ppermute x15, starting transfers between devices, per_device(): lax.ppermute(sent, ('ab', 'cd'), [(i, i ^ step) for i in range(devices)])  26.5 us
    another operation x1, local copies, waits for them, and re-layouts, per_device(): arrived = arrived.reshape(blocks, cd_size, occ_dev, group_size, group_size)  12.9 us
    another operation x1, local copies, waits for them, and re-layouts, cut_along(): shard.reshape(*dims[:dim], devices, dims[dim] // devices, *dims[dim + 1:])  12.3 us
    dot_general x1, matrix products, place_rows(): jnp.einsum('okf,kef->oke', chosen, tile_rows, precision=lax.Precision.HIG...  12.3 us
    reshape x2, local copies, waits for them, and re-layouts, per_device(): outgoing = summed.reshape(group_size, occ_dev, blocks, cd_size, group_size)  6.95 us
    transpose x1, local copies, waits for them, and re-layouts, per_device(): jnp.transpose(arrived, (2, 4, 0, 1, 3))  6.88 us
  transfers between devices with their start and end apart: 18, of which 5 were waited for; matrix products, arithmetic and copies ran while one was open for 1% of the time, Pallas kernels for 0%

profile of v1, /device:TPU:0, one launch (start us, length us, event | category | flops | bytes accessed | tf_op | source)
XLA Modules:
  0.0 168.3 jit_solution(14620065206130452820)
XLA Ops:
  6.5 1.8 %copy.13 = f32[256,256]{0,1:T(8,128)} copy(f32[256,256]{1,0:T(8,128)} %param.5) | data formatting | bytes 524288 | tf_op args[0]
  8.3 0.0 all-gather.2.cloned.1.call-update
  8.3 0.0 reduce-scatter.2.cloned.1.call-start
  9.1 0.7 compare_select_fusion.1
  9.7 0.7 compare_and_fusion
  10.4 28.0 %all-gather.2.cloned.1.call-done = f32[256,1024]{0,1:T(8,128)} async-done(((f32[256,256]{0,1:T(8,128)}), f32[256,1024]{0,1:T(8,128)}) %all-gather.2.cloned.1.call-update) | async-done | bytes 1048592 | tf_op jit(solution)/shard_map/all_gather | solution.py:51
  38.4 1.6 copy.14
  40.0 2.8 %gather_fusion = f32[16,256,256]{2,1,0:T(8,128)} fusion(f32[256,4,256]{2,0,1:T(8,128)S(1)} %copy.14, s32[1024]{0:T(1024)S(1)} %pad_clamp_fusion.1), kind=kCustom, calls=%fused_computation | custom fusion | bytes 8388672 | tf_op jit(solution)/shard_map/jit(_take)/gather | solution.py:53
  42.7 12.3 %fusion = f32[16,256,256]{1,2,0:T(8,128)S(1)} fusion(f32[16,256,256]{2,1,0:T(8,128)} %param.6, f32[16,256,256]{2,1,0:T(8,128)} %gather_fusion, pred[16]{0:T(512)(128)(4,1)S(1)} %compare_and_fusion), kind=kOutput, calls=%fused_computation.2 | convolution fusion | flops 3222274048 | bytes 12582928 | tf_op jit(solution)/shard_map/okf,kef->oke/dot_general | solution.py:31
  55.0 3.9 %fusion.7 = f32[16,256,4,16]{1,2,3,0:T(4,128)S(1)} fusion(f32[256,16,16,16]{0,3,2,1:T(8,128)S(1)} %bitcast.81, s32[16]{0:T(128)S(1)} %copy-done.1, pred[16]{0:T(512)(128)(4,1)S(1)} %iota_compare_fusion.1), kind=kOutput, calls=%fused_computation.9 | convolution fusion | flops 50331776 | bytes 5242960 | tf_op jit(solution)/shard_map/rk,okab->aorb/dot_general | solution.py:34
  58.9 1.2 copy.16
  60.1 0.0 reduce-scatter.2.cloned.1.call-update
  60.2 27.4 %reduce-scatter.2.cloned.1.call-done = f32[4,256,64]{1,2,0:T(8,128)} async-done(((f32[16,256,64]{1,2,0:T(8,128)}), f32[4,256,64]{1,2,0:T(8,128)}) %reduce-scatter.2.cloned.1.call-update) | async-done | bytes 262160 | tf_op jit(solution)/shard_map/reduce_scatter | solution.py:55
  87.6 1.0 reshape.47
  88.6 5.9 %copy.17 = f32[4,256,4,4,4]{4,0,1,3,2:T(4,128)} copy(f32[4,256,4,4,4]{1,4,3,2,0:T(4,128)S(1)} %reshape.47) | data formatting | bytes 524288 | tf_op jit(solution)/shard_map/reshape | solution.py:57
  94.5 12.3 %reshape_reshape.6 = f32[16,1,4096]{2,0,1:T(8,128)S(1)} reshape(f32[4,4,256,4,4]{4,3,2,1,0:T(4,128)} %bitcast.78) | data formatting | bytes 524288 | tf_op jit(solution)/shard_map/reshape;reshape | solution.py:10
  106.9 0.3 dynamic-slice_bitcast_fusion
  107.2 0.1 collective-permute-start
  107.3 1.4 collective-permute-start.1
  108.7 2.9 %collective-permute-start.2 = (f32[1,4096]{1,0:T(1,128)S(1)}, f32[1,4096]{1,0:T(1,128)S(1)}, u32[]{:S(2)}, u32[]{:S(2)}) collective-permute-start(f32[1,4096]{1,0:T(1,128)S(1)} %get-tuple-element.17), channel_id=1, source_target_pairs={{0,6},{2,4},{4,2},{6,0},{8,14},{10,12},{12,10},{14,8},{16,22},{18,... | collective-permute-start | bytes 49160 | tf_op jit(solution)/shard_map/ppermute | solution.py:65
  111.6 1.5 collective-permute-start.3
  113.1 0.0 collective-permute-start.4
  113.1 2.4 %collective-permute-start.5 = (f32[1,4096]{1,0:T(1,128)S(1)}, f32[1,4096]{1,0:T(1,128)S(1)}, u32[]{:S(2)}, u32[]{:S(2)}) collective-permute-start(f32[1,4096]{1,0:T(1,128)S(1)} %get-tuple-element.14), channel_id=1, source_target_pairs={{0,12},{2,14},{4,8},{6,10},{8,4},{10,6},{12,0},{14,2},{16,28},{18,... | collective-permute-start | bytes 49160 | tf_op jit(solution)/shard_map/ppermute | solution.py:65
  115.5 0.0 collective-permute-done.1
  115.5 2.9 %collective-permute-start.6 = (f32[1,4096]{1,0:T(1,128)S(1)}, f32[1,4096]{1,0:T(1,128)S(1)}, u32[]{:S(2)}, u32[]{:S(2)}) collective-permute-start(f32[1,4096]{1,0:T(1,128)S(1)} %get-tuple-element.13), channel_id=1, source_target_pairs={{0,14},{2,12},{4,10},{6,8},{8,6},{10,4},{12,2},{14,0},{16,30},{18,... | collective-permute-start | bytes 49160 | tf_op jit(solution)/shard_map/ppermute | solution.py:65
  118.4 0.0 collective-permute-done.2
  118.4 1.5 collective-permute-start.7
  119.9 0.0 collective-permute-done.3
  119.9 0.0 collective-permute-start.8
  119.9 2.4 %collective-permute-start.9 = (f32[1,4096]{1,0:T(1,128)S(1)}, f32[1,4096]{1,0:T(1,128)S(1)}, u32[]{:S(2)}, u32[]{:S(2)}) collective-permute-start(f32[1,4096]{1,0:T(1,128)S(1)} %get-tuple-element.10), channel_id=1, source_target_pairs={{0,20},{2,22},{4,16},{6,18},{8,28},{10,30},{12,24},{14,26},{16,4},... | collective-permute-start | bytes 49160 | tf_op jit(solution)/shard_map/ppermute | solution.py:65
  122.3 0.0 collective-permute-done.5
  122.3 3.0 %collective-permute-start.10 = (f32[1,4096]{1,0:T(1,128)S(1)}, f32[1,4096]{1,0:T(1,128)S(1)}, u32[]{:S(2)}, u32[]{:S(2)}) collective-permute-start(f32[1,4096]{1,0:T(1,128)S(1)} %get-tuple-element.9), channel_id=1, source_target_pairs={{0,22},{2,20},{4,18},{6,16},{8,30},{10,28},{12,26},{14,24},{16,6},... | collective-permute-start | bytes 49160 | tf_op jit(solution)/shard_map/ppermute | solution.py:65
  125.2 0.0 collective-permute-done.6
  125.2 2.4 %collective-permute-start.11 = (f32[1,4096]{1,0:T(1,128)S(1)}, f32[1,4096]{1,0:T(1,128)S(1)}, u32[]{:S(2)}, u32[]{:S(2)}) collective-permute-start(f32[1,4096]{1,0:T(1,128)S(1)} %get-tuple-element.8), channel_id=1, source_target_pairs={{0,24},{2,26},{4,28},{6,30},{8,16},{10,18},{12,20},{14,22},{16,8},... | collective-permute-start | bytes 49160 | tf_op jit(solution)/shard_map/ppermute | solution.py:65
  127.6 3.2 %collective-permute-start.13 = (f32[1,4096]{1,0:T(1,128)S(1)}, f32[1,4096]{1,0:T(1,128)S(1)}, u32[]{:S(2)}, u32[]{:S(2)}) collective-permute-start(f32[1,4096]{1,0:T(1,128)S(1)} %get-tuple-element.6), channel_id=1, source_target_pairs={{0,28},{2,30},{4,24},{6,26},{8,20},{10,22},{12,16},{14,18},{16,12}... | collective-permute-start | bytes 49160 | tf_op jit(solution)/shard_map/ppermute | solution.py:65
  130.9 0.0 collective-permute-done.9
  130.9 2.9 %collective-permute-start.14 = (f32[1,4096]{1,0:T(1,128)S(1)}, f32[1,4096]{1,0:T(1,128)S(1)}, u32[]{:S(2)}, u32[]{:S(2)}) collective-permute-start(f32[1,4096]{1,0:T(1,128)S(1)} %get-tuple-element.5), channel_id=1, source_target_pairs={{0,30},{2,28},{4,26},{6,24},{8,22},{10,20},{12,18},{14,16},{16,14}... | collective-permute-start | bytes 49160 | tf_op jit(solution)/shard_map/ppermute | solution.py:65
  133.8 0.0 collective-permute-done.11
  133.8 0.3 collective-permute-done.13
  134.1 4.1 %collective-permute-done.14 = f32[1,4096]{1,0:T(1,128)S(1)} collective-permute-done((f32[1,4096]{1,0:T(1,128)S(1)}, f32[1,4096]{1,0:T(1,128)S(1)}, u32[]{:S(2)}, u32[]{:S(2)}) %collective-permute-start.14) | collective-permute-done | bytes 16416 | tf_op jit(solution)/shard_map/ppermute | solution.py:65
  138.2 0.4 stack.63
  138.6 0.6 gather_fusion.1
  139.2 12.9 %reshape_reshape.7 = f32[4,4,256,4,4]{4,3,2,1,0:T(4,128)} reshape(f32[16,4096]{1,0:T(8,128)S(1)} %gather_fusion.1) | data formatting | bytes 524288 | tf_op jit(solution)/shard_map/reshape;reshape | solution.py:68
  152.1 6.9 %copy.18 = f32[256,4,4,4,4]{0,4,3,2,1:T(4,128)S(1)} copy(f32[256,4,4,4,4]{1,4,0,3,2:T(4,128)} %bitcast.79) | data formatting | bytes 524288 | tf_op jit(solution)/shard_map/transpose | solution.py:69
  159.0 0.1 reshape.48
  159.1 0.1 collective-permute-start.15
  159.2 1.5 collective-permute-done.15
  160.7 0.7 fusion.10
  (16 shorter events, 0.1 us)
Async XLA Ops:
  6.5 31.9 %all-gather.2.cloned.1.call-start = ((), (), s32[]{:S(2)}) async-start(), calls=%async_computation.1 | async-start | bytes 1310720 | tf_op jit(solution)/shard_map/all_gather | solution.py:51
  8.3 79.2 %reduce-scatter.2.cloned.1.call-start = ((), (), s32[]{:S(2)}) async-start(), calls=%async_computation.2 | async-start | bytes 1310720 | tf_op jit(solution)/shard_map/reduce_scatter | solution.py:55
  42.7 12.3 %copy-start.1 = (s32[16]{0:T(128)S(1)}, s32[16]{0:T(128)}, u32[]{:S(2)}) copy-start(s32[16]{0:T(128)} %param.7) | copy-start | bytes 196
  107.2 5.9 %collective-permute-start = (f32[1,4096]{1,0:T(1,128)S(1)}, f32[1,4096]{1,0:T(1,128)S(1)}, u32[]{:S(2)}, u32[]{:S(2)}) collective-permute-start(f32[1,4096]{1,0:T(1,128)S(1)} %get-tuple-element.19), channel_id=1, source_target_pairs={{0,2},{2,0},{4,6},{6,4},{8,10},{10,8},{12,14},{14,12},{16,18},{18,... | collective-permute-start | bytes 49160 | tf_op jit(solution)/shard_map/ppermute | solution.py:65
  107.3 8.2 %collective-permute-start.1 = (f32[1,4096]{1,0:T(1,128)S(1)}, f32[1,4096]{1,0:T(1,128)S(1)}, u32[]{:S(2)}, u32[]{:S(2)}) collective-permute-start(f32[1,4096]{1,0:T(1,128)S(1)} %get-tuple-element.18), channel_id=1, source_target_pairs={{0,4},{2,6},{4,0},{6,2},{8,12},{10,14},{12,8},{14,10},{16,20},{18,... | collective-permute-start | bytes 49160 | tf_op jit(solution)/shard_map/ppermute | solution.py:65
  108.7 9.7 %collective-permute-start.2 = (f32[1,4096]{1,0:T(1,128)S(1)}, f32[1,4096]{1,0:T(1,128)S(1)}, u32[]{:S(2)}, u32[]{:S(2)}) collective-permute-start(f32[1,4096]{1,0:T(1,128)S(1)} %get-tuple-element.17), channel_id=1, source_target_pairs={{0,6},{2,4},{4,2},{6,0},{8,14},{10,12},{12,10},{14,8},{16,22},{18,... | collective-permute-start | bytes 49160 | tf_op jit(solution)/shard_map/ppermute | solution.py:65
  111.6 8.2 %collective-permute-start.3 = (f32[1,4096]{1,0:T(1,128)S(1)}, f32[1,4096]{1,0:T(1,128)S(1)}, u32[]{:S(2)}, u32[]{:S(2)}) collective-permute-start(f32[1,4096]{1,0:T(1,128)S(1)} %get-tuple-element.16), channel_id=1, source_target_pairs={{0,8},{2,10},{4,12},{6,14},{8,0},{10,2},{12,4},{14,6},{16,24},{18,... | collective-permute-start | bytes 49160 | tf_op jit(solution)/shard_map/ppermute | solution.py:65
  113.1 6.8 %collective-permute-start.4 = (f32[1,4096]{1,0:T(1,128)S(1)}, f32[1,4096]{1,0:T(1,128)S(1)}, u32[]{:S(2)}, u32[]{:S(2)}) collective-permute-start(f32[1,4096]{1,0:T(1,128)S(1)} %get-tuple-element.15), channel_id=1, source_target_pairs={{0,10},{2,8},{4,14},{6,12},{8,2},{10,0},{12,6},{14,4},{16,26},{18,... | collective-permute-start | bytes 49160 | tf_op jit(solution)/shard_map/ppermute | solution.py:65
  113.1 9.2 %collective-permute-start.5 = (f32[1,4096]{1,0:T(1,128)S(1)}, f32[1,4096]{1,0:T(1,128)S(1)}, u32[]{:S(2)}, u32[]{:S(2)}) collective-permute-start(f32[1,4096]{1,0:T(1,128)S(1)} %get-tuple-element.14), channel_id=1, source_target_pairs={{0,12},{2,14},{4,8},{6,10},{8,4},{10,6},{12,0},{14,2},{16,28},{18,... | collective-permute-start | bytes 49160 | tf_op jit(solution)/shard_map/ppermute | solution.py:65
  115.5 9.8 %collective-permute-start.6 = (f32[1,4096]{1,0:T(1,128)S(1)}, f32[1,4096]{1,0:T(1,128)S(1)}, u32[]{:S(2)}, u32[]{:S(2)}) collective-permute-start(f32[1,4096]{1,0:T(1,128)S(1)} %get-tuple-element.13), channel_id=1, source_target_pairs={{0,14},{2,12},{4,10},{6,8},{8,6},{10,4},{12,2},{14,0},{16,30},{18,... | collective-permute-start | bytes 49160 | tf_op jit(solution)/shard_map/ppermute | solution.py:65
  118.4 9.2 %collective-permute-start.7 = (f32[1,4096]{1,0:T(1,128)S(1)}, f32[1,4096]{1,0:T(1,128)S(1)}, u32[]{:S(2)}, u32[]{:S(2)}) collective-permute-start(f32[1,4096]{1,0:T(1,128)S(1)} %get-tuple-element.12), channel_id=1, source_target_pairs={{0,16},{2,18},{4,20},{6,22},{8,24},{10,26},{12,28},{14,30},{16,0},... | collective-permute-start | bytes 49160 | tf_op jit(solution)/shard_map/ppermute | solution.py:65
  119.9 7.8 %collective-permute-start.8 = (f32[1,4096]{1,0:T(1,128)S(1)}, f32[1,4096]{1,0:T(1,128)S(1)}, u32[]{:S(2)}, u32[]{:S(2)}) collective-permute-start(f32[1,4096]{1,0:T(1,128)S(1)} %get-tuple-element.11), channel_id=1, source_target_pairs={{0,18},{2,16},{4,22},{6,20},{8,26},{10,24},{12,30},{14,28},{16,2},... | collective-permute-start | bytes 49160 | tf_op jit(solution)/shard_map/ppermute | solution.py:65
  119.9 11.0 %collective-permute-start.9 = (f32[1,4096]{1,0:T(1,128)S(1)}, f32[1,4096]{1,0:T(1,128)S(1)}, u32[]{:S(2)}, u32[]{:S(2)}) collective-permute-start(f32[1,4096]{1,0:T(1,128)S(1)} %get-tuple-element.10), channel_id=1, source_target_pairs={{0,20},{2,22},{4,16},{6,18},{8,28},{10,30},{12,24},{14,26},{16,4},... | collective-permute-start | bytes 49160 | tf_op jit(solution)/shard_map/ppermute | solution.py:65
  122.3 11.5 %collective-permute-start.10 = (f32[1,4096]{1,0:T(1,128)S(1)}, f32[1,4096]{1,0:T(1,128)S(1)}, u32[]{:S(2)}, u32[]{:S(2)}) collective-permute-start(f32[1,4096]{1,0:T(1,128)S(1)} %get-tuple-element.9), channel_id=1, source_target_pairs={{0,22},{2,20},{4,18},{6,16},{8,30},{10,28},{12,26},{14,24},{16,6},... | collective-permute-start | bytes 49160 | tf_op jit(solution)/shard_map/ppermute | solution.py:65
  125.2 8.6 %collective-permute-start.11 = (f32[1,4096]{1,0:T(1,128)S(1)}, f32[1,4096]{1,0:T(1,128)S(1)}, u32[]{:S(2)}, u32[]{:S(2)}) collective-permute-start(f32[1,4096]{1,0:T(1,128)S(1)} %get-tuple-element.8), channel_id=1, source_target_pairs={{0,24},{2,26},{4,28},{6,30},{8,16},{10,18},{12,20},{14,22},{16,8},... | collective-permute-start | bytes 49160 | tf_op jit(solution)/shard_map/ppermute | solution.py:65
  127.6 6.2 %collective-permute-start.12 = (f32[1,4096]{1,0:T(1,128)S(1)}, f32[1,4096]{1,0:T(1,128)S(1)}, u32[]{:S(2)}, u32[]{:S(2)}) collective-permute-start(f32[1,4096]{1,0:T(1,128)S(1)} %get-tuple-element.7), channel_id=1, source_target_pairs={{0,26},{2,24},{4,30},{6,28},{8,18},{10,16},{12,22},{14,20},{16,10}... | collective-permute-start | bytes 49160 | tf_op jit(solution)/shard_map/ppermute | solution.py:65
  127.6 6.5 %collective-permute-start.13 = (f32[1,4096]{1,0:T(1,128)S(1)}, f32[1,4096]{1,0:T(1,128)S(1)}, u32[]{:S(2)}, u32[]{:S(2)}) collective-permute-start(f32[1,4096]{1,0:T(1,128)S(1)} %get-tuple-element.6), channel_id=1, source_target_pairs={{0,28},{2,30},{4,24},{6,26},{8,20},{10,22},{12,16},{14,18},{16,12}... | collective-permute-start | bytes 49160 | tf_op jit(solution)/shard_map/ppermute | solution.py:65
  130.9 7.3 %collective-permute-start.14 = (f32[1,4096]{1,0:T(1,128)S(1)}, f32[1,4096]{1,0:T(1,128)S(1)}, u32[]{:S(2)}, u32[]{:S(2)}) collective-permute-start(f32[1,4096]{1,0:T(1,128)S(1)} %get-tuple-element.5), channel_id=1, source_target_pairs={{0,30},{2,28},{4,26},{6,24},{8,22},{10,20},{12,18},{14,16},{16,14}... | collective-permute-start | bytes 49160 | tf_op jit(solution)/shard_map/ppermute | solution.py:65
  152.1 8.6 %copy-start = (f32[4,256,64]{1,2,0:T(8,128)S(1)}, f32[4,256,64]{1,2,0:T(8,128)}, u32[]{:S(2)}) copy-start(f32[4,256,64]{1,2,0:T(8,128)} %reduce-scatter.2.cloned.1.call-done) | copy-start | bytes 786436
  159.1 1.6 collective-permute-start.15
Sparse Core Ops, SparseCore 0:
  9.2 29.2 all-gather.1
  60.2 27.3 reduce-scatter.1
